TPU v7x, 32 devices: a whole 2x2x4 slice. The times are simulated.
32 devices in a mesh: station: 4 (over z), group: 4 (over x, core), bias: 2 (over y).
Axes of the slice: x: 2, y: 2, z: 4, core: 2. Of those that a mesh axis runs over, the one named last changes fastest.
Arguments:
- normal_mat: float32 [128, 2304], P(('station', 'group')), may hold values from -16 to 18, as said below
- coupling: float32 [128, 2, 8, 48, 128], P(('station', 'group'), 'bias'), may hold values from -0.13258252 to 0.13258252
- lengths: int32 [128], P(('station', 'group')), may hold values from 12 to 48
- visible: int32 [128, 2, 8], P(('station', 'group'), 'bias'), may hold values from 0 to 16, as said below
- bias_prior: float32 [2, 16, 128], P('bias', 'station'), may hold values from 0.1 to 1
- unimod: int32 [128, 2304], P(('station', 'group')), may hold values from -1 to 2, as said below
Outputs:
- bias_cov: float32 [2, 16, 128, 128], P('bias', 'station')
- amb_cov: float32 [128, 2304], P(('station', 'group'))
Inputs may be any that keep to these rules, and one draw needn't show every extreme that they name: `normal_mat`: each station's matrix, read as 48 x 48 row by row, is symmetric with all eigenvalues 1 or more. Each list visible[s, h] holds distinct block numbers below 16 in its first slots and the value 16 in its unused slots; every list has at least one block; in every draw the stations of some devices use all 8 slots. `unimod`: each station's matrix, read as 48 x 48 row by row, is a unit lower triangular times a unit upper triangular integer matrix; each row of the lower factor and each column of the upper factor holds at most one entry off the diagonal, -1 or 1; so every leading square block has determinant 1.
All inputs are finite; a program needn't handle non-finite values.
Results may differ from a plain program's by a relative error of at most 0.0003.
Values sent between devices are 32-bit elements; how exact they have to be, the bound alone decides.
No kernel may reach another device: no remote copies, remote signals or barrier semaphores. Data moves between devices by JAX's collectives and lax.ppermute only.
A program may use at most 64 MiB of HBM per device.

v0:
```python
import jax
import jax.numpy as jnp
from jax import lax
from jax.sharding import PartitionSpec as P

NHALF = 16
precise = lax.Precision.HIGHEST


def spd_inverse(matrix):
    matrix_order = matrix.shape[-1]
    factor = jnp.linalg.cholesky(matrix)
    identity = jnp.broadcast_to(jnp.eye(matrix_order, dtype=matrix.dtype), matrix.shape)
    lower_inv = lax.linalg.triangular_solve(factor, identity, left_side=True, lower=True)
    return jnp.einsum("...ka,...kb->...ab", lower_inv, lower_inv, precision=precise)


def prepare(normal_mat, coupling, lengths):
    stations = coupling.shape[0]
    block_len = coupling.shape[3]
    positions = jnp.arange(block_len, dtype=jnp.int32)
    row_valid = (positions[None, :] < lengths[:, None]).astype(jnp.float32)
    keep_mask = row_valid[:, :, None] * row_valid[:, None, :]
    stacked = normal_mat.reshape(stations, block_len, block_len)
    effective = keep_mask * stacked + (1.0 - keep_mask) * jnp.eye(block_len, dtype=jnp.float32)
    inverse = spd_inverse(effective)
    weighted = coupling * row_valid[:, None, None, :, None]
    solved = jnp.einsum("sab,shjbc->shjac", inverse, weighted, precision=precise)
    return (keep_mask, inverse, weighted, solved)


def finish_cov(keep_mask, inverse, bias_part, unimod):
    stations = keep_mask.shape[0]
    block_len = keep_mask.shape[1]
    covariance = keep_mask * (inverse + bias_part)
    integer_map = unimod.reshape(stations, block_len, block_len).astype(jnp.float32)
    mapped = jnp.einsum("sab,sbc,sdc->sad", integer_map, covariance, integer_map, precision=precise)
    return (keep_mask * mapped).reshape(stations, block_len * block_len)


def local(normal_mat, coupling, lengths, visible, bias_prior, unimod):
    keep_mask, inverse, weighted, solved = prepare(normal_mat, coupling, lengths)
    reduced = jnp.einsum("shjac,shjad->shjcd", weighted, weighted - solved, precision=precise)
    block_width = coupling.shape[4]
    identity = jnp.eye(block_width, dtype=jnp.float32)
    columns = jnp.arange(NHALF, dtype=jnp.int32)
    selector = (visible[..., None] == columns).astype(jnp.float32)
    block_table = jnp.einsum("shjx,shjcd->hxcd", selector, reduced, precision=precise)
    local_sum = lax.psum_scatter(block_table, "station", scatter_dimension=1, tiled=True)
    block_sum = lax.psum(local_sum, "group")
    bias_cov = spd_inverse(block_sum + bias_prior[..., :, None] * identity)
    segment = lax.all_gather(bias_cov, "station", axis=1, tiled=True)
    piece_len = segment.shape[1]
    local_pick = (visible[..., None] == jnp.arange(piece_len, dtype=jnp.int32)).astype(jnp.float32)
    chosen = jnp.einsum("shjx,hxcd->shjcd", local_pick, segment, precision=precise)
    lifted = jnp.einsum("shjac,shjcd->shjad", solved, chosen, precision=precise)
    bias_part = jnp.einsum("shjad,shjbd->sab", lifted, solved, precision=precise)
    combined = lax.psum(bias_part.reshape(bias_part.shape[0], -1), "bias")
    amb_cov = finish_cov(keep_mask, inverse, combined.reshape(bias_part.shape), unimod)
    return (bias_cov, amb_cov)


def solution(mesh):
    return jax.shard_map(
        local,
        mesh=mesh,
        in_specs=(
            P(("station", "group"), None),
            P(("station", "group"), "bias", None, None, None),
            P(("station", "group")),
            P(("station", "group"), "bias", None),
            P("bias", "station", None),
            P(("station", "group"), None),
        ),
        out_specs=(P("bias", "station", None, None), P(("station", "group"), None)),
        check_vma=False,
    )
```

profile of v0, /device:TPU:0, one launch (start us, length us, event | category | flops | bytes accessed | tf_op | source)
XLA Modules:
  0.0 314.8 jit_solution(5613608994066356341)
XLA Ops:
  7.3 0.7 fusion.43
  8.1 1.0 reshape.177
  9.6 35.2 %custom-call.14 = f32[8,48,48]{2,1,0:T(8,128)S(1)} custom-call(f32[8,48,48]{2,1,0:T(8,128)S(1)} %fusion.30), custom_call_target="Cholesky" | custom-call | tf_op jit(solution)/shard_map/jit(cholesky)/cholesky | solution.py:12
  45.0 29.5 %custom-call.15 = f32[8,1,48,48]{2,3,1,0:T(8,128)S(1)} custom-call(f32[8,1,48,48]{3,2,1,0:T(8,128)S(1)} %select_bitcast_fusion.1), custom_call_target="InvertDiagBlocksLowerTriangular" | custom-call | tf_op jit(solution)/shard_map/triangular_solve | solution.py:14
  74.6 0.5 fusion.28
  75.6 1.7 fusion.10
  77.3 6.9 %fusion.7 = f32[8,8,128,128]{3,2,1,0:T(8,128)S(1)} fusion(f32[8,8,128,48]{2,3,1,0:T(8,128)S(1)} %fusion.10, f32[8,1,8,48,128]{4,3,2,1,0:T(8,128)S(1)} %copy-done, f32[8,48]{1,0:T(8,128)S(1)} %fusion.43), kind=kOutput, calls=%fused_computation.9 | convolution fusion | flops 605159424 | bytes 7341568 | tf_op jit(solution)/shard_map/shjac,shjad->shjcd/dot_general | solution.py:43
  84.2 4.1 %fusion.12 = f32[16,128,128]{2,0,1:T(8,128)S(1)} fusion(f32[8,8,128,128]{3,2,1,0:T(8,128)S(1)} %fusion.7, s32[8,8]{1,0:T(8,128)S(1)} %bitcast.86), kind=kOutput, calls=%fused_computation.14 | convolution fusion | flops 201327616 | bytes 5243136 | tf_op jit(solution)/shard_map/shjx,shjcd->hxcd/dot_general | solution.py:48
  88.3 1.4 copy.62
  89.9 30.1 %reduce-scatter.2.cloned.1.call-done = f32[1,4,128,128]{2,3,1,0:T(8,128)} async-done(((f32[1,16,128,128]{2,3,1,0:T(8,128)}), f32[1,4,128,128]{2,3,1,0:T(8,128)}) %reduce-scatter.2.cloned.1.call-update) | async-done | bytes 262160 | tf_op jit(solution)/shard_map/reduce_scatter | solution.py:49
  120.2 32.9 %all-reduce.3.cloned.1.call-done = f32[1,4,128,128]{2,3,1,0:T(8,128)} async-done(((f32[1,4,128,128]{2,3,1,0:T(8,128)}), f32[1,4,128,128]{2,3,1,0:T(8,128)}) %all-reduce.3.cloned.1.call-update) | async-done | bytes 262160 | tf_op jit(solution)/shard_map/psum | solution.py:50
  153.1 1.0 multiply_add_fusion
  154.2 1.0 fusion.23
  155.3 46.9 %custom-call.16 = f32[1,4,128,128]{3,2,1,0:T(8,128)S(1)} custom-call(f32[1,4,128,128]{3,2,1,0:T(8,128)S(1)} %fusion.23), custom_call_target="Cholesky" | custom-call | tf_op jit(solution)/shard_map/jit(cholesky)/cholesky | solution.py:12
  202.4 39.3 %custom-call.17 = f32[1,4,1,128,128]{3,4,2,1,0:T(8,128)S(1)} custom-call(f32[1,4,1,128,128]{4,3,2,1,0:T(8,128)S(1)} %select_bitcast_fusion), custom_call_target="InvertDiagBlocksLowerTriangular" | custom-call | tf_op jit(solution)/shard_map/triangular_solve | solution.py:14
  241.8 0.6 fusion.21
  242.3 1.3 fusion.45
  243.9 27.9 %all-gather.3.cloned.1.call-done = f32[16,128,128]{2,1,0:T(8,128)} async-done(((f32[4,128,128]{2,1,0:T(8,128)}), f32[16,128,128]{2,1,0:T(8,128)}) %all-gather.3.cloned.1.call-update) | async-done | bytes 1048592 | tf_op jit(solution)/shard_map/all_gather | solution.py:52
  271.8 3.3 %convolution_bitcast_fusion = f32[8,8,128,128]{3,1,0,2:T(8,128)S(1)} fusion(f32[16,128,128,1]{2,1,0,3:T(8,128)} %bitcast.85, s32[8,8]{1,0:T(8,128)S(1)} %bitcast.87), kind=kOutput, calls=%fused_computation.4 | convolution fusion | flops 201327616 | bytes 5243136 | tf_op jit(solution)/shard_map/shjx,hxcd->shjcd/dot_general | solution.py:55
  275.1 6.0 %fusion = f32[8,8,48,128]{3,2,1,0:T(8,128)S(1)} fusion(f32[8,8,128,48]{2,3,1,0:T(8,128)S(1)} %fusion.10, f32[8,8,128,128]{3,1,0,2:T(8,128)S(1)} %convolution_bitcast_fusion), kind=kOutput, calls=%fused_computation | convolution fusion | flops 603979776 | bytes 7340032 | tf_op jit(solution)/shard_map/shjac,shjcd->shjad/dot_general | solution.py:56
  281.1 2.4 fusion.15
  283.8 21.7 %all-reduce.5.cloned.1.call-done = f32[8,48,48]{1,2,0:T(8,128)} async-done(((f32[8,48,48]{1,2,0:T(8,128)}), f32[8,48,48]{1,2,0:T(8,128)}) %all-reduce.5.cloned.1.call-update) | async-done | bytes 73744 | tf_op jit(solution)/shard_map/psum | solution.py:58
  305.5 1.4 fusion.26
  307.5 0.8 reshape.185
  (41 shorter events, 3.1 us)
Async XLA Ops:
  7.2 112.8 %reduce-scatter.2.cloned.1.call-start = ((), (), s32[]{:S(2)}) async-start(), calls=%async_computation.1 | async-start | bytes 1310720 | tf_op jit(solution)/shard_map/reduce_scatter | solution.py:49
  9.2 66.4 %copy-start = (f32[8,1,8,48,128]{4,3,2,1,0:T(8,128)S(1)}, f32[8,1,8,48,128]{4,3,2,1,0:T(8,128)}, u32[]{:S(2)}) copy-start(f32[8,1,8,48,128]{4,3,2,1,0:T(8,128)} %param.7) | copy-start | bytes 4718596
  77.3 6.9 %copy-start.2 = (s32[8,1,8]{2,1,0:T(1,128)S(1)}, s32[8,1,8]{2,1,0:T(1,128)}, u32[]{:S(2)}) copy-start(s32[8,1,8]{2,1,0:T(1,128)} %param.9) | copy-start | bytes 772
  88.3 64.8 %copy-start.3 = (f32[1,4,128]{2,1,0:T(4,128)S(1)}, f32[1,4,128]{2,1,0:T(4,128)}, u32[]{:S(2)}) copy-start(f32[1,4,128]{2,1,0:T(4,128)} %param.10) | copy-start | bytes 6148
  89.8 63.3 %all-reduce.3.cloned.1.call-start = ((), (), s32[]{:S(2)}) async-start(), calls=%async_computation.2 | async-start | bytes 524288 | tf_op jit(solution)/shard_map/psum | solution.py:50
  120.0 151.8 %all-gather.3.cloned.1.call-start = ((), (), s32[]{:S(2)}) async-start(), calls=%async_computation.4 | async-start | bytes 1310720 | tf_op jit(solution)/shard_map/all_gather | solution.py:52
  243.7 61.8 %all-reduce.5.cloned.1.call-start = ((), (), s32[]{:S(2)}) async-start(), calls=%async_computation.3 | async-start | bytes 393216 | tf_op jit(solution)/shard_map/psum | solution.py:58
  281.1 2.5 copy-start.1
Sparse Core Ops, SparseCore 0:
  89.9 29.9 reduce-scatter.1
  122.3 30.7 all-reduce.2
  243.8 27.9 all-gather.2
  283.6 21.7 all-reduce.4
where the time goes:
time: 315 us
  other arithmetic  154 us (49%)
  waiting for transfers between devices  113 us (36%)
  matrix products  29.1 us (9%)
  between operations  14.1 us (4%)
  local copies, waits for them, and re-layouts  4.08 us (1%)
    another operation x8, other arithmetic, spd_inverse(): factor = jnp.linalg.cholesky(matrix)  82.4 us
    another operation x6, other arithmetic, spd_inverse(): lax.linalg.triangular_solve(factor, identity, left_side=True, lower=True)  69.1 us
    psum x1, waiting for transfers between devices, local(): block_sum = lax.psum(local_sum, 'group')  32.9 us
    reduce_scatter x1, waiting for transfers between devices, local(): lax.psum_scatter(block_table, 'station', scatter_dimension=1, tiled=True)  30.1 us
    all_gather x1, waiting for transfers between devices, local(): segment = lax.all_gather(bias_cov, 'station', axis=1, tiled=True)  27.9 us
    psum x1, waiting for transfers between devices, local(): combined = lax.psum(bias_part.reshape(bias_part.shape[0], -1), 'bias')  21.7 us
    dot_general x1, matrix products, local(): jnp.einsum('shjac,shjad->shjcd', weighted, weighted - solved, precision=p...  6.89 us
  transfers between devices with their start and end apart: 4, of which 4 were waited for; matrix products, arithmetic and copies ran while one was open for 0% of the time, Pallas kernels for 0%

commit v1 on v0

--- a/solution.py
+++ b/solution.py
@@ -49,7 +49,7 @@
     local_sum = lax.psum_scatter(block_table, "station", scatter_dimension=1, tiled=True)
     block_sum = lax.psum(local_sum, "group")
     bias_cov = spd_inverse(block_sum + bias_prior[..., :, None] * identity)
-    segment = lax.all_gather(bias_cov, "station", axis=1, tiled=True)
+    segment = jnp.concatenate(lax.all_gather(bias_cov, "station"), axis=1)
     piece_len = segment.shape[1]
     local_pick = (visible[..., None] == jnp.arange(piece_len, dtype=jnp.int32)).astype(jnp.float32)
     chosen = jnp.einsum("shjx,hxcd->shjcd", local_pick, segment, precision=precise)

time: 315 us -> 315 us (level)
  no operation moved by 1% of the time
where the time goes in v1:
time: 315 us
  other arithmetic  154 us (49%)
  waiting for transfers between devices  113 us (36%)
  matrix products  29.1 us (9%)
  between operations  14.1 us (4%)
  local copies, waits for them, and re-layouts  4.08 us (1%)
    another operation x8, other arithmetic, spd_inverse(): factor = jnp.linalg.cholesky(matrix)  82.4 us
    another operation x6, other arithmetic, spd_inverse(): lax.linalg.triangular_solve(factor, identity, left_side=True, lower=True)  69.1 us
    psum x1, waiting for transfers between devices, local(): block_sum = lax.psum(local_sum, 'group')  32.9 us
    reduce_scatter x1, waiting for transfers between devices, local(): lax.psum_scatter(block_table, 'station', scatter_dimension=1, tiled=True)  30.1 us
    all_gather x1, waiting for transfers between devices, local(): segment = jnp.concatenate(lax.all_gather(bias_cov, 'station'), axis=1)  27.9 us
    psum x1, waiting for transfers between devices, local(): combined = lax.psum(bias_part.reshape(bias_part.shape[0], -1), 'bias')  21.7 us
    dot_general x1, matrix products, local(): jnp.einsum('shjac,shjad->shjcd', weighted, weighted - solved, precision=p...  6.89 us
  transfers between devices with their start and end apart: 4, of which 4 were waited for; matrix products, arithmetic and copies ran while one was open for 0% of the time, Pallas kernels for 0%

profile of v1, /device:TPU:0, one launch (start us, length us, event | category | flops | bytes accessed | tf_op | source)
XLA Modules:
  0.0 314.8 jit_solution(5613608994066356341)
XLA Ops:
  7.3 0.7 fusion.43
  8.1 1.0 reshape.180
  9.6 35.2 %custom-call.14 = f32[8,48,48]{2,1,0:T(8,128)S(1)} custom-call(f32[8,48,48]{2,1,0:T(8,128)S(1)} %fusion.30), custom_call_target="Cholesky" | custom-call | tf_op jit(solution)/shard_map/jit(cholesky)/cholesky | solution.py:12
  45.0 29.5 %custom-call.15 = f32[8,1,48,48]{2,3,1,0:T(8,128)S(1)} custom-call(f32[8,1,48,48]{3,2,1,0:T(8,128)S(1)} %select_bitcast_fusion.1), custom_call_target="InvertDiagBlocksLowerTriangular" | custom-call | tf_op jit(solution)/shard_map/triangular_solve | solution.py:14
  74.6 0.5 fusion.28
  75.6 1.7 fusion.10
  77.3 6.9 %fusion.7 = f32[8,8,128,128]{3,2,1,0:T(8,128)S(1)} fusion(f32[8,8,128,48]{2,3,1,0:T(8,128)S(1)} %fusion.10, f32[8,1,8,48,128]{4,3,2,1,0:T(8,128)S(1)} %copy-done, f32[8,48]{1,0:T(8,128)S(1)} %fusion.43), kind=kOutput, calls=%fused_computation.9 | convolution fusion | flops 605159424 | bytes 7341568 | tf_op jit(solution)/shard_map/shjac,shjad->shjcd/dot_general | solution.py:43
  84.2 4.1 %fusion.12 = f32[16,128,128]{2,0,1:T(8,128)S(1)} fusion(f32[8,8,128,128]{3,2,1,0:T(8,128)S(1)} %fusion.7, s32[8,8]{1,0:T(8,128)S(1)} %bitcast.86), kind=kOutput, calls=%fused_computation.14 | convolution fusion | flops 201327616 | bytes 5243136 | tf_op jit(solution)/shard_map/shjx,shjcd->hxcd/dot_general | solution.py:48
  88.3 1.4 copy.62
  89.9 30.1 %reduce-scatter.2.cloned.1.call-done = f32[1,4,128,128]{2,3,1,0:T(8,128)} async-done(((f32[1,16,128,128]{2,3,1,0:T(8,128)}), f32[1,4,128,128]{2,3,1,0:T(8,128)}) %reduce-scatter.2.cloned.1.call-update) | async-done | bytes 262160 | tf_op jit(solution)/shard_map/reduce_scatter | solution.py:49
  120.2 32.9 %all-reduce.3.cloned.1.call-done = f32[1,4,128,128]{2,3,1,0:T(8,128)} async-done(((f32[1,4,128,128]{2,3,1,0:T(8,128)}), f32[1,4,128,128]{2,3,1,0:T(8,128)}) %all-reduce.3.cloned.1.call-update) | async-done | bytes 262160 | tf_op jit(solution)/shard_map/psum | solution.py:50
  153.1 1.0 multiply_add_fusion
  154.2 1.0 fusion.23
  155.3 46.9 %custom-call.16 = f32[1,4,128,128]{3,2,1,0:T(8,128)S(1)} custom-call(f32[1,4,128,128]{3,2,1,0:T(8,128)S(1)} %fusion.23), custom_call_target="Cholesky" | custom-call | tf_op jit(solution)/shard_map/jit(cholesky)/cholesky | solution.py:12
  202.4 39.3 %custom-call.17 = f32[1,4,1,128,128]{3,4,2,1,0:T(8,128)S(1)} custom-call(f32[1,4,1,128,128]{4,3,2,1,0:T(8,128)S(1)} %select_bitcast_fusion), custom_call_target="InvertDiagBlocksLowerTriangular" | custom-call | tf_op jit(solution)/shard_map/triangular_solve | solution.py:14
  241.8 0.6 fusion.21
  242.3 1.3 fusion.45
  243.9 27.9 %all-gather.3.cloned.1.call-done = f32[16,128,128]{2,1,0:T(8,128)} async-done(((f32[4,128,128]{2,1,0:T(8,128)}), f32[16,128,128]{2,1,0:T(8,128)}) %all-gather.3.cloned.1.call-update) | async-done | bytes 1048592 | tf_op jit(solution)/shard_map/all_gather | solution.py:52
  271.8 3.3 %convolution_bitcast_fusion = f32[8,8,128,128]{3,1,0,2:T(8,128)S(1)} fusion(f32[16,128,128,1]{2,1,0,3:T(8,128)} %bitcast.85, s32[8,8]{1,0:T(8,128)S(1)} %bitcast.87), kind=kOutput, calls=%fused_computation.4 | convolution fusion | flops 201327616 | bytes 5243136 | tf_op jit(solution)/shard_map/shjx,hxcd->shjcd/dot_general | solution.py:55
  275.1 6.0 %fusion = f32[8,8,48,128]{3,2,1,0:T(8,128)S(1)} fusion(f32[8,8,128,48]{2,3,1,0:T(8,128)S(1)} %fusion.10, f32[8,8,128,128]{3,1,0,2:T(8,128)S(1)} %convolution_bitcast_fusion), kind=kOutput, calls=%fused_computation | convolution fusion | flops 603979776 | bytes 7340032 | tf_op jit(solution)/shard_map/shjac,shjcd->shjad/dot_general | solution.py:56
  281.1 2.4 fusion.15
  283.8 21.7 %all-reduce.5.cloned.1.call-done = f32[8,48,48]{1,2,0:T(8,128)} async-done(((f32[8,48,48]{1,2,0:T(8,128)}), f32[8,48,48]{1,2,0:T(8,128)}) %all-reduce.5.cloned.1.call-update) | async-done | bytes 73744 | tf_op jit(solution)/shard_map/psum | solution.py:58
  305.5 1.4 fusion.26
  307.5 0.8 reshape.188
  (41 shorter events, 3.1 us)
Async XLA Ops:
  7.2 112.8 %reduce-scatter.2.cloned.1.call-start = ((), (), s32[]{:S(2)}) async-start(), calls=%async_computation.1 | async-start | bytes 1310720 | tf_op jit(solution)/shard_map/reduce_scatter | solution.py:49
  9.2 66.4 %copy-start = (f32[8,1,8,48,128]{4,3,2,1,0:T(8,128)S(1)}, f32[8,1,8,48,128]{4,3,2,1,0:T(8,128)}, u32[]{:S(2)}) copy-start(f32[8,1,8,48,128]{4,3,2,1,0:T(8,128)} %param.7) | copy-start | bytes 4718596
  77.3 6.9 %copy-start.2 = (s32[8,1,8]{2,1,0:T(1,128)S(1)}, s32[8,1,8]{2,1,0:T(1,128)}, u32[]{:S(2)}) copy-start(s32[8,1,8]{2,1,0:T(1,128)} %param.9) | copy-start | bytes 772
  88.3 64.8 %copy-start.3 = (f32[1,4,128]{2,1,0:T(4,128)S(1)}, f32[1,4,128]{2,1,0:T(4,128)}, u32[]{:S(2)}) copy-start(f32[1,4,128]{2,1,0:T(4,128)} %param.10) | copy-start | bytes 6148
  89.8 63.3 %all-reduce.3.cloned.1.call-start = ((), (), s32[]{:S(2)}) async-start(), calls=%async_computation.2 | async-start | bytes 524288 | tf_op jit(solution)/shard_map/psum | solution.py:50
  120.0 151.8 %all-gather.3.cloned.1.call-start = ((), (), s32[]{:S(2)}) async-start(), calls=%async_computation.4 | async-start | bytes 1310720 | tf_op jit(solution)/shard_map/all_gather | solution.py:52
  243.7 61.8 %all-reduce.5.cloned.1.call-start = ((), (), s32[]{:S(2)}) async-start(), calls=%async_computation.3 | async-start | bytes 393216 | tf_op jit(solution)/shard_map/psum | solution.py:58
  281.1 2.5 copy-start.1
Sparse Core Ops, SparseCore 0:
  89.9 29.9 reduce-scatter.1
  122.3 30.7 all-reduce.2
  243.8 27.9 all-gather.2
  283.6 21.7 all-reduce.4
